TPU v7x, 512 devices: a whole 4x4x16 slice. The times are simulated.
512 devices in a mesh: tm: 128 (over x_lo, z, y), feat: 4 (over x_hi, core).
Axes of the slice: x: 4 (x_hi: 2, x_lo: 2; x = x_hi * 2 + x_lo), y: 4, z: 16, core: 2. Of those that a mesh axis runs over, the one named last changes fastest.
Arguments:
- frames: bfloat16 [4096, 2048], P('tm'), may hold values from -6 to 6
- frequency: bfloat16 [2048, 4096], P(None, 'feat'), may hold values from -0.125 to 0.125
- phases: float32 [4096], P('feat'), may hold values from -3.140625 to 3.140625
Outputs:
- instant_tiles: float32 [128, 4, 128, 256], P('tm', 'feat')
- lagged_tiles: float32 [128, 4, 128, 256], P('tm', 'feat')
All inputs are finite; a program needn't handle non-finite values.
Results may differ from a plain program's by a relative error of at most 0.0003.
Values may be sent and summed in bfloat16 or wider, within the bound.
A program may use at most 64 MiB of HBM per device.

v0:
```python
import math

import jax
import jax.numpy as jnp
from jax import lax
from jax.sharding import PartitionSpec as P

LAG = 512
ROW_SPLIT = 8


SCALE = math.sqrt(2.0)


def shards(frames, frequency, phases):
    tm_count = lax.axis_size("tm")
    feat_count = lax.axis_size("feat")
    projected = jnp.dot(frames, frequency, preferred_element_type=jnp.float32) + phases[None, :]
    local_feats = (SCALE * jnp.cos(projected)).astype(jnp.bfloat16)
    frame_count, local_width = local_feats.shape
    feat_width = local_width * feat_count
    tile_rows = feat_width // (feat_count * ROW_SPLIT)
    tile_cols = feat_width * ROW_SPLIT // tm_count
    col_groups = tm_count // ROW_SPLIT
    frame_total = frame_count * tm_count
    all_feats = lax.all_gather(local_feats, "feat", axis=1, tiled=True)
    row_parts = local_feats.reshape(frame_count, ROW_SPLIT, tile_rows).transpose(1, 0, 2)
    row_send = jnp.broadcast_to(row_parts[None], (col_groups, ROW_SPLIT, frame_count, tile_rows))
    row_send = row_send.reshape(tm_count, frame_count, tile_rows)
    row_recv = lax.all_to_all(row_send, "tm", split_axis=0, concat_axis=0, tiled=True).reshape(
        frame_total, tile_rows
    )
    head_rows = row_recv[: frame_total - LAG]
    row_total = all_feats.shape[0]
    col_parts = all_feats.reshape(row_total, col_groups, tile_cols).transpose(1, 0, 2)
    spread_out = jnp.broadcast_to(col_parts[:, None], (col_groups, ROW_SPLIT, row_total, tile_cols))
    received = lax.all_to_all(
        spread_out.reshape(tm_count, row_total, tile_cols),
        "tm",
        split_axis=0,
        concat_axis=0,
        tiled=True,
    )
    col_data = received.reshape(frame_total, received.shape[2])
    instant = (
        jnp.einsum("sr,sc->rc", row_recv, col_data, preferred_element_type=jnp.float32)
        / frame_total
    )
    lagged = jnp.einsum(
        "sr,sc->rc", head_rows, col_data[LAG:], preferred_element_type=jnp.float32
    ) / (frame_total - LAG)
    instant, lagged = (instant, lagged)
    return (instant.reshape(1, 1, tile_rows, tile_cols), lagged.reshape(1, 1, tile_rows, tile_cols))


def solution(mesh):
    placed = (P("tm", None), P(None, "feat"), P("feat"))
    return jax.shard_map(
        shards,
        mesh=mesh,
        in_specs=placed,
        out_specs=(P("tm", "feat", None, None), P("tm", "feat", None, None)),
        check_vma=False,
    )
```

profile of v0, /device:TPU:4, one launch (start us, length us, event | category | flops | bytes accessed | tf_op | source)
XLA Modules:
  0.0 197.1 jit_solution(6521872163242553725)
XLA Ops:
  0.6 0.0 copy-start
  0.6 0.9 copy-done
  1.5 3.4 %fusion.15 = bf16[32,1024]{1,0:T(8,128)(2,1)S(1)} fusion(bf16[32,2048]{1,0:T(8,128)(2,1)S(1)} %copy-done, bf16[2048,1024]{1,0:T(8,128)(2,1)} %param.4, f32[1024]{0:T(1024)} %param.5), kind=kOutput, calls=%fused_computation.11 | convolution fusion | flops 134316032 | bytes 4395008 | tf_op jit(solution)/shard_map/dot_general | solution.py:18
  5.0 1.2 broadcast_in_dim.4
  6.2 20.6 %all-to-all-start = ((bf16[128,32,128]{2,1,0:T(8,128)(2,1)}), bf16[128,32,128]{2,1,0:T(8,128)(2,1)S(1)}, u32[]{:S(2)}, u32[]{:S(2)}) async-start(bf16[128,32,128]{2,1,0:T(8,128)(2,1)} %bitcast.1), calls=%async_computation | async-start | bytes 2097152 | tf_op jit(solution)/shard_map/all_to_all | solution.py:30
  26.8 7.5 %all_gather.3 = bf16[32,4096]{1,0:T(8,128)(2,1)S(1)} all-gather(bf16[32,1024]{1,0:T(8,128)(2,1)S(1)} %fusion.15), channel_id=1, replica_groups=mesh['tm'=128,'feat'=4] {'feat'}, dimensions={1}, use_global_device_ids=true | all-gather | bytes 327680 | tf_op jit(solution)/shard_map/all_gather | solution.py:26
  34.3 0.1 copy.11
  34.4 49.9 %all-to-all-done = bf16[128,32,128]{2,1,0:T(8,128)(2,1)S(1)} async-done(((bf16[128,32,128]{2,1,0:T(8,128)(2,1)}), bf16[128,32,128]{2,1,0:T(8,128)(2,1)S(1)}, u32[]{:S(2)}, u32[]{:S(2)}) %all-to-all-start) | async-done | bytes 1048608 | tf_op jit(solution)/shard_map/all_to_all | solution.py:30
  84.3 0.0 copy-start.1
  84.3 1.7 broadcast_in_dim.5
  86.0 6.2 %all-to-all-start.1 = ((bf16[128,32,256]{2,1,0:T(8,128)(2,1)}), bf16[128,32,256]{2,1,0:T(8,128)(2,1)S(1)}, u32[]{:S(2)}, u32[]{:S(2)}) async-start(bf16[128,32,256]{2,1,0:T(8,128)(2,1)} %bitcast.30), calls=%async_computation.1 | async-start | bytes 4194304 | tf_op jit(solution)/shard_map/all_to_all | solution.py:37
  92.2 0.0 copy-done.1
  92.2 0.0 slice-start
  92.2 100.4 %all-to-all-done.1 = bf16[128,32,256]{2,1,0:T(8,128)(2,1)S(1)} async-done(((bf16[128,32,256]{2,1,0:T(8,128)(2,1)}), bf16[128,32,256]{2,1,0:T(8,128)(2,1)S(1)}, u32[]{:S(2)}, u32[]{:S(2)}) %all-to-all-start.1) | async-done | bytes 2097184 | tf_op jit(solution)/shard_map/all_to_all | solution.py:37
  192.6 0.1 slice.11
  192.8 0.0 slice-done
  192.8 0.0 copy-start.2
  192.8 3.1 %fusion.12 = f32[1,1,128,256]{3,2,1,0:T(8,128)} fusion(bf16[112,32,256]{2,1,0:T(8,128)(2,1)S(1)} %slice.11, bf16[112,32,128]{2,1,0:T(8,128)(2,1)S(1)} %slice-done), kind=kOutput, calls=%fused_computation.10 | convolution fusion | flops 234913792 | bytes 2883584 | tf_op jit(solution)/shard_map/sr,sc->rc/dot_general | solution.py:49
  195.9 0.0 copy-done.2
  195.9 1.2 fusion.8
  (3 shorter events, 0.1 us)
Async XLA Ops:
  0.6 0.9 copy-start
  6.2 78.2 %all-to-all-start = ((bf16[128,32,128]{2,1,0:T(8,128)(2,1)}), bf16[128,32,128]{2,1,0:T(8,128)(2,1)S(1)}, u32[]{:S(2)}, u32[]{:S(2)}) async-start(bf16[128,32,128]{2,1,0:T(8,128)(2,1)} %bitcast.1), calls=%async_computation | async-start | bytes 2097152 | tf_op jit(solution)/shard_map/all_to_all | solution.py:30
  84.3 7.9 %copy-start.1 = (bf16[128,32,128]{2,1,0:T(8,128)(2,1)}, bf16[128,32,128]{2,1,0:T(8,128)(2,1)S(1)}, u32[]{:S(2)}) copy-start(bf16[128,32,128]{2,1,0:T(8,128)(2,1)S(1)} %all-to-all-done) | copy-start | bytes 3145732
  86.0 106.6 %all-to-all-start.1 = ((bf16[128,32,256]{2,1,0:T(8,128)(2,1)}), bf16[128,32,256]{2,1,0:T(8,128)(2,1)S(1)}, u32[]{:S(2)}, u32[]{:S(2)}) async-start(bf16[128,32,256]{2,1,0:T(8,128)(2,1)} %bitcast.30), calls=%async_computation.1 | async-start | bytes 4194304 | tf_op jit(solution)/shard_map/all_to_all | solution.py:37
  92.2 100.6 %slice-start = ((bf16[128,32,128]{2,1,0:T(8,128)(2,1)}), bf16[112,32,128]{2,1,0:T(8,128)(2,1)S(1)}, s32[]{:S(2)}) async-start(bf16[128,32,128]{2,1,0:T(8,128)(2,1)} %copy-done.1), calls=%async_computation.2 | async-start | bytes 1835008 | tf_op jit(solution)/shard_map/slice | solution.py:33
  192.8 3.1 %copy-start.2 = (bf16[128,32,128]{2,1,0:T(8,128)(2,1)S(1)}, bf16[128,32,128]{2,1,0:T(8,128)(2,1)}, u32[]{:S(2)}) copy-start(bf16[128,32,128]{2,1,0:T(8,128)(2,1)} %copy-done.1) | copy-start | bytes 3145732
where the time goes:
time: 197 us
  waiting for transfers between devices  150 us (76%)
  starting transfers between devices  26.8 us (14%)
  matrix products  7.72 us (4%)
  blocking collectives  7.49 us (4%)
  local copies, waits for them, and re-layouts  4.04 us (2%)
    all_to_all x1, waiting for transfers between devices, shards(): lax.all_to_all(spread_out.reshape(tm_count, row_total, tile_cols), 'tm',...  100 us
    all_to_all x1, waiting for transfers between devices, shards(): lax.all_to_all(row_send, 'tm', split_axis=0, concat_axis=0, tiled=True)  49.9 us
    all_to_all x1, starting transfers between devices, shards(): lax.all_to_all(row_send, 'tm', split_axis=0, concat_axis=0, tiled=True)  20.6 us
    all_gather x1, blocking collectives, shards(): all_feats = lax.all_gather(local_feats, 'feat', axis=1, tiled=True)  7.49 us
    all_to_all x1, starting transfers between devices, shards(): lax.all_to_all(spread_out.reshape(tm_count, row_total, tile_cols), 'tm',...  6.21 us
  transfers between devices with their start and end apart: 2, of which 2 were waited for; matrix products, arithmetic and copies ran while one was open for 0% of the time, Pallas kernels for 0%

commit v1 on v0

v1 whole, which is shorter than its diff:
```python
import math

import jax
import jax.numpy as jnp
from jax import lax
from jax.sharding import Mesh, PartitionSpec as P

LAG = 512
SCALE = math.sqrt(2.0)
G, K = 16, 8


def shards(frames, frequency, phases):
    feat_count = lax.axis_size("feat")
    projected = jnp.dot(frames, frequency, preferred_element_type=jnp.float32) + phases[None, :]
    feats = (SCALE * jnp.cos(projected)).astype(jnp.bfloat16)
    count, width = feats.shape
    rows = width // K
    cols = width * feat_count // G
    total = count * G * K
    part = count // feat_count
    r = feats.reshape(count, K, rows).transpose(1, 0, 2)
    r = lax.all_to_all(r, "k", split_axis=0, concat_axis=0, tiled=True)
    r = lax.all_gather(r.reshape(K * count, rows), "g", axis=0, tiled=False)
    c = feats.reshape(feat_count, part, width)
    c = lax.all_to_all(c, "feat", split_axis=0, concat_axis=0, tiled=True)
    c = c.reshape(feat_count, part, G // feat_count, cols).transpose(0, 2, 1, 3)
    c = c.reshape(G, part, cols)
    c = lax.all_to_all(c, "g", split_axis=0, concat_axis=0, tiled=True)
    c = lax.all_gather(c, ("k", "feat"), axis=1, tiled=False)
    c = c.reshape(total, cols)
    r = r.reshape(total, rows)
    instant = jnp.einsum("sr,sc->rc", r, c, preferred_element_type=jnp.float32) / total
    lagged = jnp.einsum(
        "sr,sc->rc", r[: total - LAG], c[LAG:], preferred_element_type=jnp.float32
    ) / (total - LAG)
    return instant.reshape(1, 1, rows, cols), lagged.reshape(1, 1, rows, cols)


def solution(mesh):
    fine = Mesh(mesh.devices.reshape(G, K, mesh.shape["feat"]), ("g", "k", "feat"))
    tm = ("g", "k")
    return jax.shard_map(
        shards,
        mesh=fine,
        in_specs=(P(tm, None), P(None, "feat"), P("feat")),
        out_specs=(P(tm, "feat", None, None), P(tm, "feat", None, None)),
        check_vma=False,
    )
```

time: 197 us -> 193 us (0.980)
  the two profiles are of different devices: /device:TPU:4 before, /device:TPU:1 now
where the time goes in v1:
time: 193 us
  waiting for transfers between devices  120 us (62%)
  blocking collectives  48.6 us (25%)
  between operations  14.1 us (7%)
  matrix products  7.5 us (4%)
  local copies, waits for them, and re-layouts  2.35 us (1%)
    all_gather x1, waiting for transfers between devices, shards(): c = lax.all_gather(c, ('k', 'feat'), axis=1, tiled=False)  79 us
    all_gather x1, waiting for transfers between devices, shards(): r = lax.all_gather(r.reshape(K * count, rows), 'g', axis=0, tiled=False)  41 us
    all_to_all x1, blocking collectives, shards(): c = lax.all_to_all(c, 'g', split_axis=0, concat_axis=0, tiled=True)  25.2 us
    all_to_all x1, blocking collectives, shards(): c = lax.all_to_all(c, 'feat', split_axis=0, concat_axis=0, tiled=True)  11.9 us
    all_to_all x1, blocking collectives, shards(): r = lax.all_to_all(r, 'k', split_axis=0, concat_axis=0, tiled=True)  11.5 us
  transfers between devices with their start and end apart: 2, of which 2 were waited for; matrix products, arithmetic and copies ran while one was open for 1% of the time, Pallas kernels for 0%

profile of v1, /device:TPU:1, one launch (start us, length us, event | category | flops | bytes accessed | tf_op | source)
XLA Modules:
  0.0 192.7 jit_solution(4748888414658896848)
XLA Ops:
  7.2 0.0 copy-start
  7.2 0.0 all-gather.4.cloned.1.call-start
  7.2 0.8 copy-done
  8.1 3.4 %fusion.4 = bf16[32,1024]{1,0:T(8,128)(2,1)S(1)} fusion(bf16[32,2048]{1,0:T(8,128)(2,1)S(1)} %copy-done, bf16[2048,1024]{1,0:T(8,128)(2,1)} %param.4, f32[1024]{0:T(1024)} %param.5), kind=kOutput, calls=%fused_computation.7 | convolution fusion | flops 134316032 | bytes 4395008 | tf_op jit(solution)/shard_map/dot_general | solution.py:15
  11.5 11.5 %all_to_all.15 = bf16[8,32,128]{2,1,0:T(8,128)(2,1)} all-to-all(bf16[8,32,128]{2,1,0:T(8,128)(2,1)S(1)} %bitcast_bitcast_fusion), channel_id=1, replica_groups=mesh['g'=16,'k'=8,'feat'=4] {'k'}, dimensions={0} | all-to-all | bytes 131072 | tf_op jit(solution)/shard_map/all_to_all | solution.py:23
  23.0 0.0 all-gather.4.cloned.1.call-update
  23.0 0.0 all-gather.6.cloned.1.call-start
  23.1 11.9 %all_to_all.16 = bf16[4,8,1024]{2,1,0:T(8,128)(2,1)S(1)} all-to-all(bf16[4,8,1024]{2,1,0:T(8,128)(2,1)S(1)} %bitcast.28), channel_id=1, replica_groups=mesh['g'=16,'k'=8,'feat'=4] {'feat'}, dimensions={0} | all-to-all | bytes 131072 | tf_op jit(solution)/shard_map/all_to_all | solution.py:26
  35.0 25.2 %all_to_all.17 = bf16[16,8,256]{2,1,0:T(8,128)(2,1)} all-to-all(bf16[16,8,256]{2,1,0:T(8,128)(2,1)S(1)} %bitcast.30), channel_id=1, replica_groups=mesh['g'=16,'k'=8,'feat'=4] {'g'}, dimensions={0} | all-to-all | bytes 131072 | tf_op jit(solution)/shard_map/all_to_all | solution.py:29
  60.2 0.0 all-gather.6.cloned.1.call-update
  60.2 41.0 %all-gather.4.cloned.1.call-done = bf16[16,256,128]{2,1,0:T(8,128)(2,1)} async-done(((bf16[1,256,128]{2,1,0:T(8,128)(2,1)}), bf16[16,256,128]{2,1,0:T(8,128)(2,1)}) %all-gather.4.cloned.1.call-update) | async-done | bytes 1048592 | tf_op jit(solution)/shard_map/all_gather | solution.py:24
  101.2 0.0 copy-start.2
  101.2 1.3 slice.37
  102.6 79.0 %all-gather.6.cloned.1.call-done = bf16[16,256,256]{2,1,0:T(8,128)(2,1)} async-done(((bf16[16,8,256]{2,1,0:T(8,128)(2,1)}), bf16[16,256,256]{2,1,0:T(8,128)(2,1)}) %all-gather.6.cloned.1.call-update) | async-done | bytes 2097168 | tf_op jit(solution)/shard_map/all_gather | solution.py:30
  181.6 0.0 copy-start.1
  181.6 0.0 copy-done.2
  181.6 2.9 %fusion.3 = f32[1,1,128,256]{3,2,1,0:T(8,128)} fusion(bf16[4096,128]{1,0:T(8,128)(2,1)S(1)} %bitcast.26, bf16[4096,256]{1,0:T(8,128)(2,1)} %bitcast.24), kind=kOutput, calls=%fused_computation.6 | convolution fusion | flops 268468224 | bytes 3276800 | tf_op jit(solution)/shard_map/sr,sc->rc/dot_general | solution.py:33
  184.5 0.0 copy-done.1
  184.5 0.1 slice.38
  184.6 1.2 fusion
  (3 shorter events, 0.0 us)
Async XLA Ops:
  7.2 0.9 copy-start
  7.2 94.0 %all-gather.4.cloned.1.call-start = ((), (), s32[]{:S(2)}) async-start(), calls=%async_computation.3 | async-start | bytes 1114112 | tf_op jit(solution)/shard_map/all_gather | solution.py:24
  23.0 158.6 %all-gather.6.cloned.1.call-start = ((), (), s32[]{:S(2)}) async-start(), calls=%async_computation.4 | async-start | bytes 2162688 | tf_op jit(solution)/shard_map/all_gather | solution.py:30
  101.2 80.4 %copy-start.2 = (bf16[16,256,128]{2,1,0:T(8,128)(2,1)S(1)}, bf16[16,256,128]{2,1,0:T(8,128)(2,1)}, u32[]{:S(2)}) copy-start(bf16[16,256,128]{2,1,0:T(8,128)(2,1)} %all-gather.4.cloned.1.call-done) | copy-start | bytes 3145732
  181.6 2.9 %copy-start.1 = (bf16[16,256,256]{2,1,0:T(8,128)(2,1)S(1)}, bf16[16,256,256]{2,1,0:T(8,128)(2,1)}, u32[]{:S(2)}) copy-start(bf16[16,256,256]{2,1,0:T(8,128)(2,1)} %all-gather.6.cloned.1.call-done) | copy-start | bytes 6291460
Sparse Core Ops, SparseCore 0:
  23.1 78.0 all-gather.3
  103.3 78.2 all-gather.5

commit v2 on v1

v2 whole, which is shorter than its diff:
```python
import math

import jax
import jax.numpy as jnp
from jax import lax
from jax.experimental import pallas as pl
from jax.experimental.pallas import tpu as pltpu
from jax.sharding import Mesh, PartitionSpec as P

SCALE = math.sqrt(2.0)
MESH = pl.DeviceIdType.MESH
AXES = ("xl", "zz", "zp", "y", "xh", "co")
SHAPE = (2, 8, 2, 4, 2, 2)
FRAMES, LAG = 4096, 512
NSEND = 40


def kernel(feats, inst, lagd, rows, cols, send, rsem, zsem, xsem, csem, ysem, osem):
    xl, zz, zp, y, xh, co = (lax.axis_index(a) for a in AXES)
    par, zq, up = zz % 2, zz // 2, zz // 4
    me_k = zp * 4 + y
    own = jnp.logical_and(jnp.logical_and(xl == xh, co == par), co == up)
    sends = []

    def remote(src, dst, sem, **dev):
        copy = pltpu.make_async_remote_copy(
            src_ref=src,
            dst_ref=dst,
            send_sem=send.at[len(sends)],
            recv_sem=sem,
            device_id=dev,
            device_id_type=MESH,
        )
        sends.append(copy)
        return copy

    def arrived(ref, sem):
        pltpu.make_async_copy(ref, ref, sem).wait()

    barrier = pltpu.get_barrier_semaphore()

    def greet(**dev):
        pl.semaphore_signal(barrier, inc=1, device_id=dev, device_id_type=MESH)

    for q in range(4):
        @pl.when(jnp.logical_not(jnp.logical_and(own, zq == q)))
        def _():
            greet(xl=xh, xh=xl, zz=2 * q + co, co=up)
    for d in range(1, 8):
        k = (me_k + d) % 8
        greet(zp=k // 4, y=k % 4)
    above, below = (zz + 1) % 8, (zz + 7) % 8
    greet(zz=above)
    greet(zz=below)
    greet(xl=1 - xl)
    greet(xh=1 - xh)
    greet(co=1 - co)
    pl.semaphore_wait(barrier, 16 - own.astype(jnp.int32))

    for k in range(8):
        src = feats.at[:, 128 * k : 128 * (k + 1)]
        dst = rows.at[y, par, xl, zq, zp]
        copy = remote(src, dst, rsem, zp=k // 4, y=k % 4)
        local = pltpu.make_async_copy(src, dst, rsem)
        pl.when(me_k != k)(copy.start)
        pl.when(me_k == k)(local.start)
    for j in range(4):
        src = feats.at[:, 256 * j : 256 * (j + 1)]
        dst = cols.at[y, par, xl, zq, zp]
        mine = jnp.logical_and(own, zz == 4 * co + j)
        copy = remote(src, dst, csem.at[0], xl=xh, xh=xl, zz=4 * co + j, co=par)
        local = pltpu.make_async_copy(src, dst, csem.at[0])
        pl.when(jnp.logical_not(mine))(copy.start)
        pl.when(mine)(local.start)

    def block(z):
        return rows.at[:, z % 2, xl, z // 2]

    def ring(z, sem, **dev):
        remote(block(z), block(z), sem, **dev).start()

    arrived(block(zz), rsem)
    ring(zz, zsem.at[0, 0], zz=above)
    ring(zz, zsem.at[1, 0], zz=below)
    ring(zz, xsem, xl=1 - xl)

    def step(s):
        lo, hi = (zz + 8 - s) % 8, (zz + s) % 8
        arrived(block(lo), zsem.at[0, s - 1])
        if s < 3:
            ring(lo, zsem.at[0, s], zz=above)
        else:
            half = rows.at[0:2, lo % 2, xl, lo // 2]
            remote(half, half, zsem.at[0, s], zz=above).start()
        arrived(block(hi), zsem.at[1, s - 1])
        if s < 3:
            ring(hi, zsem.at[1, s], zz=below)
        else:
            half = rows.at[2:4, hi % 2, xl, hi // 2]
            remote(half, half, zsem.at[1, s], zz=below).start()
        ring(lo, xsem, xl=1 - xl)
        ring(hi, xsem, xl=1 - xl)

    part = cols.at[y, co, xh, :, zp]
    arrived(part, csem.at[0])
    remote(part, part, csem.at[1], xh=1 - xh).start()
    step(1)
    arrived(cols.at[y, co, 1 - xh, :, zp], csem.at[1])
    part = cols.at[y, co, :, :, zp]
    remote(part, part, csem.at[2], zp=1 - zp).start()
    step(2)
    arrived(cols.at[y, co, :, :, 1 - zp], csem.at[2])
    nxt, prv, opp = (y + 1) % 4, (y + 3) % 4, (y + 2) % 4
    for h in range(2):
        up_half, down_half = cols.at[y, co, h], cols.at[y, co, 1 - h]
        remote(up_half, up_half, ysem.at[0, h], y=nxt).start()
        remote(down_half, down_half, ysem.at[1, 1 - h], y=prv).start()

    def other(v):
        remote(cols.at[v, co], cols.at[v, co], osem, co=1 - co).start()

    other(y)
    step(3)
    arrived(cols.at[prv, co, 0], ysem.at[0, 0])
    far = cols.at[prv, co, 0]
    remote(far, far, ysem.at[0, 2], y=nxt).start()
    arrived(cols.at[nxt, co, 1], ysem.at[1, 1])
    far = cols.at[nxt, co, 1]
    remote(far, far, ysem.at[1, 2], y=prv).start()
    last = (zz + 4) % 8
    arrived(rows.at[0:2, last % 2, xl, last // 2], zsem.at[0, 3])
    arrived(rows.at[2:4, last % 2, xl, last // 2], zsem.at[1, 3])
    ring(last, xsem, xl=1 - xl)
    arrived(cols.at[prv, co, 1], ysem.at[0, 1])
    other(prv)
    arrived(cols.at[nxt, co, 0], ysem.at[1, 0])
    other(nxt)
    arrived(cols.at[opp, co, 0], ysem.at[0, 2])
    arrived(cols.at[opp, co, 1], ysem.at[1, 2])
    other(opp)
    arrived(rows.at[:, :, 1 - xl], xsem)
    arrived(cols.at[:, 1 - co], osem)

    over = (((0,), (0,)), ((), ()))

    def body(i, carry):
        total, late = carry
        r = rows[i // 2, i % 2].reshape(512, 128)
        c = cols[i // 2, i % 2].reshape(512, 256)
        total += lax.dot_general(r, c, over, preferred_element_type=jnp.float32)
        late += lax.dot_general(r[:448], c[64:], over, preferred_element_type=jnp.float32)
        return total, late

    zero = jnp.zeros(inst.shape, jnp.float32)
    total, late = lax.fori_loop(0, 8, body, (zero, zero))
    inst[...] = total / FRAMES
    lagd[...] = late / (FRAMES - LAG)

    for k, copy in enumerate(sends[:8]):
        pl.when(me_k != k)(copy.wait_send)
    for j, copy in enumerate(sends[8:12]):
        mine = jnp.logical_and(own, zz == 4 * co + j)
        pl.when(jnp.logical_not(mine))(copy.wait_send)
    for copy in sends[12:]:
        copy.wait_send()


def shards(frames, frequency, phases):
    projected = jnp.dot(frames, frequency, preferred_element_type=jnp.float32) + phases[None, :]
    feats = (SCALE * jnp.cos(projected)).astype(jnp.bfloat16)
    vmem = pl.BlockSpec(memory_space=pltpu.VMEM)
    dma = pltpu.SemaphoreType.DMA
    tile = jax.ShapeDtypeStruct((128, 256), jnp.float32)
    inst, lagd = pl.pallas_call(
        kernel,
        out_shape=(tile, tile),
        in_specs=[vmem],
        out_specs=(vmem, vmem),
        scratch_shapes=[
            pltpu.VMEM((4, 2, 2, 4, 2, 32, 128), jnp.bfloat16),
            pltpu.VMEM((4, 2, 2, 4, 2, 32, 256), jnp.bfloat16),
            dma((NSEND,)),
            dma,
            dma((2, 4)),
            dma,
            dma((3,)),
            dma((2, 3)),
            dma,
        ],
        compiler_params=pltpu.CompilerParams(collective_id=0, has_side_effects=True),
    )(feats)
    return inst[None, None], lagd[None, None]


def solution(mesh):
    fine = Mesh(mesh.devices.reshape(SHAPE), AXES)
    tm, feat = AXES[:4], AXES[4:]
    return jax.shard_map(
        shards,
        mesh=fine,
        in_specs=(P(tm, None), P(None, feat), P(feat)),
        out_specs=(P(tm, feat, None, None), P(tm, feat, None, None)),
        check_vma=False,
    )
```

time: 193 us -> 58 us (0.30)
  waiting for transfers between devices: 120 us -> 0 us
  Pallas kernels: 0 us -> 49.1 us
  blocking collectives: 48.6 us -> 0 us
  between operations: 14.1 us -> 0.65 us
  matrix products: 7.5 us -> 4.06 us
    all_gather x2 -> x0, waiting for transfers between devices: 120 us -> none  [the longest x1 79 us: shards(): c = lax.all_gather(c, ('k', 'feat'), axis=1, tiled=False)]
    pallas_call x0 -> x1, Pallas kernels: none -> 49.1 us  [shards(): pl.pallas_call(kernel, out_shape=(tile, tile), in_specs=[vmem], out_specs...]
    all_to_all x3 -> x0, blocking collectives: 48.6 us -> none  [the longest x1 25.2 us: shards(): c = lax.all_to_all(c, 'g', split_axis=0, concat_axis=0, tiled=True)]
    dot_general x2 -> x0, matrix products: 4.07 us -> none  [the longest x1 2.91 us: shards(): jnp.einsum('sr,sc->rc', r, c, preferred_element_type=jnp.float32) / total]
    unnamed x6 -> x4, local copies, waits for them, and re-layouts: 0.86 us -> 4.04 us
  transfers between devices with their start and end apart: 2 -> 0, of which waited for: 2 -> 0; matrix products, arithmetic and copies ran while one was open for 1% -> 0% of each run, Pallas kernels for 0% -> 0%
where the time goes in v2:
time: 58 us; the launch traced here: 57.8 us
  Pallas kernels  49.1 us (85%)
  matrix products  4.06 us (7%)
  local copies, waits for them, and re-layouts  4.04 us (7%)
  between operations  0.65 us (1%)
    pallas_call x1, Pallas kernels, shards(): pl.pallas_call(kernel, out_shape=(tile, tile), in_specs=[vmem], out_specs...  49.1 us
    dot_general x1, matrix products, shards(): jnp.dot(frames, frequency, preferred_element_type=jnp.float32)  4.06 us
    unnamed x4, local copies, waits for them, and re-layouts  4.04 us

profile of v2, /device:TPU:1, one launch (start us, length us, event | category | flops | bytes accessed | tf_op | source)
XLA Modules:
  0.0 57.8 jit_solution(10853752152740724835)
XLA Ops:
  0.6 0.0 copy-start
  0.6 0.9 %copy-done = bf16[32,2048]{1,0:T(8,128)(2,1)S(1)} copy-done((bf16[32,2048]{1,0:T(8,128)(2,1)S(1)}, bf16[32,2048]{1,0:T(8,128)(2,1)}, u32[]{:S(2)}) %copy-start) | copy-done | bytes 131096
  1.5 4.1 %fusion.2.feats = bf16[32,1024]{1,0:T(8,128)(2,1)} fusion(bf16[32,2048]{1,0:T(8,128)(2,1)S(1)} %copy-done, bf16[2048,1024]{1,0:T(8,128)(2,1)} %param.4, f32[1024]{0:T(1024)} %param.5), kind=kOutput, calls=%fused_computation.3 | convolution fusion | flops 134316032 | bytes 4395008 | tf_op jit(solution)/shard_map/dot_general | solution.py:169
  5.6 49.1 %shard_map.50 = (f32[128,256]{1,0:T(8,128)}, f32[128,256]{1,0:T(8,128)}) custom-call(bf16[32,1024]{1,0:T(8,128)(2,1)} %fusion.2.feats), custom_call_target="tpu_custom_call" | custom-call | tf_op jit(solution)/shard_map/pallas_call | solution.py:174
  54.7 1.6 %copy.7 = f32[1,1,128,256]{3,2,1,0:T(8,128)} copy(f32[1,1,128,256]{3,2,1,0:T(8,128)} %bitcast.5) | data formatting | bytes 262144
  56.3 1.6 %copy.8 = f32[1,1,128,256]{3,2,1,0:T(8,128)} copy(f32[1,1,128,256]{3,2,1,0:T(8,128)} %bitcast.4) | data formatting | bytes 262144
Async XLA Ops:
  0.6 0.9 %copy-start = (bf16[32,2048]{1,0:T(8,128)(2,1)S(1)}, bf16[32,2048]{1,0:T(8,128)(2,1)}, u32[]{:S(2)}) copy-start(bf16[32,2048]{1,0:T(8,128)(2,1)} %param.3) | copy-start | bytes 393220

commit v3 on v2

v3 whole, which is shorter than its diff:
```python
import math

import jax
import jax.numpy as jnp
from jax import lax
from jax.experimental import pallas as pl
from jax.experimental.pallas import tpu as pltpu
from jax.sharding import Mesh, PartitionSpec as P

SCALE = math.sqrt(2.0)
MESH = pl.DeviceIdType.MESH
AXES = ("xl", "zz", "zp", "y", "xh", "co")
SHAPE = (2, 8, 2, 4, 2, 2)
FRAMES, LAG = 4096, 512
NSEND = 99
VMEM = 24 * 2**20


def kernel(feats, inst, lagd, rows, cols, send, rsem, zsem, xsem, csem, hsem, ysem, osem):
    xl, zz, zp, y, xh, co = (lax.axis_index(a) for a in AXES)
    par, zq, up = zz % 2, zz // 2, zz // 4
    me_k = zp * 4 + y
    own = jnp.logical_and(jnp.logical_and(xl == xh, co == par), co == up)
    sends = []

    def remote(src, dst, sem, **dev):
        copy = pltpu.make_async_remote_copy(
            src_ref=src,
            dst_ref=dst,
            send_sem=send.at[len(sends)],
            recv_sem=sem,
            device_id=dev,
            device_id_type=MESH,
        )
        sends.append(copy)
        return copy

    def arrived(ref, sem):
        pltpu.make_async_copy(ref, ref, sem).wait()

    barrier = pltpu.get_barrier_semaphore()

    def greet(**dev):
        pl.semaphore_signal(barrier, inc=1, device_id=dev, device_id_type=MESH)

    for q in range(4):
        @pl.when(jnp.logical_not(jnp.logical_and(own, zq == q)))
        def _():
            greet(xl=xh, xh=xl, zz=2 * q + co, co=up)
    for d in range(1, 8):
        k = (me_k + d) % 8
        greet(zp=k // 4, y=k % 4)
    above, below = (zz + 1) % 8, (zz + 7) % 8
    greet(zz=above)
    greet(zz=below)
    greet(xl=1 - xl)
    greet(xh=1 - xh)
    greet(co=1 - co)
    pl.semaphore_wait(barrier, 16 - own.astype(jnp.int32))

    for k in range(8):
        src = feats.at[:, 128 * k : 128 * (k + 1)]
        dst = rows.at[y, par, xl, zq, zp]
        copy = remote(src, dst, rsem.at[y], zp=k // 4, y=k % 4)
        local = pltpu.make_async_copy(src, dst, rsem.at[y])
        pl.when(me_k != k)(copy.start)
        pl.when(me_k == k)(local.start)
    for j in range(4):
        src = feats.at[:, 256 * j : 256 * (j + 1)]
        dst = cols.at[y, par, xl, zq, zp]
        mine = jnp.logical_and(own, zz == 4 * co + j)
        copy = remote(src, dst, csem.at[zq], xl=xh, xh=xl, zz=4 * co + j, co=par)
        local = pltpu.make_async_copy(src, dst, csem.at[zq])
        pl.when(jnp.logical_not(mine))(copy.start)
        pl.when(mine)(local.start)

    def push(ref, sem, **dev):
        remote(ref, ref, sem, **dev).start()

    def chunk(z, d):
        return rows.at[(y + d) % 4, z % 2, xl, z // 2]

    def across(z):
        push(rows.at[:, z % 2, xl, z // 2], xsem, xl=1 - xl)

    def row_start():
        for d in range(4):
            v = (y + d) % 4
            arrived(chunk(zz, d), rsem.at[v])
            push(chunk(zz, d), zsem.at[0, 0, d], zz=above)
            push(chunk(zz, d), zsem.at[1, 0, d], zz=below)
        across(zz)

    def row_step(s):
        lo, hi = (zz + 8 - s) % 8, (zz + s) % 8
        for d in range(4):
            arrived(chunk(lo, d), zsem.at[0, s - 1, d])
            if s < 3 or d < 2:
                push(chunk(lo, d), zsem.at[0, s, d], zz=above)
            arrived(chunk(hi, d), zsem.at[1, s - 1, d])
            if s < 3 or d >= 2:
                push(chunk(hi, d), zsem.at[1, s, d], zz=below)
        across(lo)
        across(hi)

    def row_last():
        last = (zz + 4) % 8
        for d in range(4):
            arrived(chunk(last, d), zsem.at[d // 2, 3, d])
            push(chunk(last, d), xsem, xl=1 - xl)

    nxt, prv, opp = (y + 1) % 4, (y + 3) % 4, (y + 2) % 4
    piece = [(zq + d) % 4 for d in (0, 1, 3, 2)]

    def other(v, p):
        push(cols.at[v, co, :, piece[p]], osem, co=1 - co)

    def col_x(p):
        q = piece[p]
        arrived(cols.at[y, co, xh, q, zp], csem.at[q])
        push(cols.at[y, co, xh, q, zp], hsem.at[0, p], xh=1 - xh)

    def col_z(p):
        q = piece[p]
        arrived(cols.at[y, co, 1 - xh, q, zp], hsem.at[0, p])
        push(cols.at[y, co, :, q, zp], hsem.at[1, p], zp=1 - zp)

    def col_y(p):
        q = piece[p]
        arrived(cols.at[y, co, :, q, 1 - zp], hsem.at[1, p])
        for h in range(2):
            push(cols.at[y, co, h, q], ysem.at[0, p, h], y=nxt)
            push(cols.at[y, co, 1 - h, q], ysem.at[1, p, 1 - h], y=prv)
        other(y, p)

    def col_far(p):
        q = piece[p]
        arrived(cols.at[prv, co, 0, q], ysem.at[0, p, 0])
        push(cols.at[prv, co, 0, q], ysem.at[0, p, 2], y=nxt)
        arrived(cols.at[nxt, co, 1, q], ysem.at[1, p, 1])
        push(cols.at[nxt, co, 1, q], ysem.at[1, p, 2], y=prv)
        arrived(cols.at[prv, co, 1, q], ysem.at[0, p, 1])
        other(prv, p)
        arrived(cols.at[nxt, co, 0, q], ysem.at[1, p, 0])
        other(nxt, p)

    def col_last(p):
        q = piece[p]
        arrived(cols.at[opp, co, 0, q], ysem.at[0, p, 2])
        arrived(cols.at[opp, co, 1, q], ysem.at[1, p, 2])
        other(opp, p)

    row_start()
    col_x(0)
    col_x(1)
    col_x(2)
    row_step(1)
    col_z(0)
    col_x(3)
    col_z(1)
    col_z(2)
    col_y(0)
    row_step(2)
    col_z(3)
    col_y(1)
    col_y(2)
    col_far(0)
    row_step(3)
    col_y(3)
    col_far(1)
    col_far(2)
    col_last(0)
    row_last()
    col_far(3)
    for p in range(1, 4):
        col_last(p)
    arrived(rows.at[:, :, 1 - xl], xsem)
    arrived(cols.at[:, 1 - co], osem)

    over = (((0,), (0,)), ((), ()))

    def body(i, carry):
        total, late = carry
        r = rows[i // 2, i % 2].reshape(512, 128)
        c = cols[i // 2, i % 2].reshape(512, 256)
        total += lax.dot_general(r, c, over, preferred_element_type=jnp.float32)
        late += lax.dot_general(r[:448], c[64:], over, preferred_element_type=jnp.float32)
        return total, late

    zero = jnp.zeros(inst.shape, jnp.float32)
    total, late = lax.fori_loop(0, 8, body, (zero, zero))
    inst[...] = total / FRAMES
    lagd[...] = late / (FRAMES - LAG)

    for k, copy in enumerate(sends[:8]):
        pl.when(me_k != k)(copy.wait_send)
    for j, copy in enumerate(sends[8:12]):
        mine = jnp.logical_and(own, zz == 4 * co + j)
        pl.when(jnp.logical_not(mine))(copy.wait_send)
    assert len(sends) == NSEND
    for copy in sends[12:]:
        copy.wait_send()


def shards(frames, frequency, phases):
    projected = jnp.dot(frames, frequency, preferred_element_type=jnp.float32) + phases[None, :]
    feats = (SCALE * jnp.cos(projected)).astype(jnp.bfloat16)
    vmem = pl.BlockSpec(memory_space=pltpu.VMEM)
    dma = pltpu.SemaphoreType.DMA
    tile = jax.ShapeDtypeStruct((128, 256), jnp.float32)
    inst, lagd = pl.pallas_call(
        kernel,
        out_shape=(tile, tile),
        in_specs=[vmem],
        out_specs=(vmem, vmem),
        scratch_shapes=[
            pltpu.VMEM((4, 2, 2, 4, 2, 32, 128), jnp.bfloat16),
            pltpu.VMEM((4, 2, 2, 4, 2, 32, 256), jnp.bfloat16),
            dma((NSEND,)),
            dma((4,)),
            dma((2, 4, 4)),
            dma,
            dma((4,)),
            dma((2, 4)),
            dma((2, 4, 3)),
            dma,
        ],
        compiler_params=pltpu.CompilerParams(collective_id=0, has_side_effects=True, vmem_limit_bytes=VMEM),
    )(feats)
    return inst[None, None], lagd[None, None]


def solution(mesh):
    fine = Mesh(mesh.devices.reshape(SHAPE), AXES)
    tm, feat = AXES[:4], AXES[4:]
    return jax.shard_map(
        shards,
        mesh=fine,
        in_specs=(P(tm, None), P(None, feat), P(feat)),
        out_specs=(P(tm, feat, None, None), P(tm, feat, None, None)),
        check_vma=False,
    )
```

time: 58 us -> 52.6 us (0.907)
  Pallas kernels: 49.1 us -> 46.2 us
  local copies, waits for them, and re-layouts: 4.04 us -> 2.22 us
  matrix products: 4.06 us -> 3.42 us
    pallas_call x1, Pallas kernels: 49.1 us -> 46.2 us  [shards(): pl.pallas_call(kernel, out_shape=(tile, tile), in_specs=[vmem], out_specs...]
    unnamed x4, local copies, waits for them, and re-layouts: 4.04 us -> 2.22 us
    dot_general x1, matrix products: 4.06 us -> 3.42 us  [shards(): jnp.dot(frames, frequency, preferred_element_type=jnp.float32)]
where the time goes in v3:
time: 52.6 us; the launch traced here: 52.5 us
  Pallas kernels  46.2 us (88%)
  matrix products  3.42 us (7%)
  local copies, waits for them, and re-layouts  2.22 us (4%)
  between operations  0.65 us (1%)
    pallas_call x1, Pallas kernels, shards(): pl.pallas_call(kernel, out_shape=(tile, tile), in_specs=[vmem], out_specs...  46.2 us
    dot_general x1, matrix products, shards(): jnp.dot(frames, frequency, preferred_element_type=jnp.float32)  3.42 us
    unnamed x4, local copies, waits for them, and re-layouts  2.22 us

profile of v3, /device:TPU:1, one launch (start us, length us, event | category | flops | bytes accessed | tf_op | source)
XLA Modules:
  0.0 52.5 jit_solution(12096545060278123100)
XLA Ops:
  0.6 0.0 copy-start
  0.6 0.9 %copy-done = bf16[32,2048]{1,0:T(8,128)(2,1)S(1)} copy-done((bf16[32,2048]{1,0:T(8,128)(2,1)S(1)}, bf16[32,2048]{1,0:T(8,128)(2,1)}, u32[]{:S(2)}) %copy-start) | copy-done | bytes 131096
  1.5 3.4 %fusion.2.feats = bf16[32,1024]{1,0:T(8,128)(2,1)S(1)} fusion(bf16[32,2048]{1,0:T(8,128)(2,1)S(1)} %copy-done, bf16[2048,1024]{1,0:T(8,128)(2,1)} %param.4, f32[1024]{0:T(1024)} %param.5), kind=kOutput, calls=%fused_computation.3 | convolution fusion | flops 134316032 | bytes 4395008 | tf_op jit(solution)/shard_map/dot_general | solution.py:206
  5.0 46.2 %shard_map.50 = (f32[128,256]{1,0:T(8,128)S(1)}, f32[128,256]{1,0:T(8,128)S(1)}) custom-call(bf16[32,1024]{1,0:T(8,128)(2,1)S(1)} %fusion.2.feats), custom_call_target="tpu_custom_call" | custom-call | tf_op jit(solution)/shard_map/pallas_call | solution.py:211
  51.2 0.7 %copy.7 = f32[1,1,128,256]{3,2,1,0:T(8,128)} copy(f32[1,1,128,256]{3,2,1,0:T(8,128)S(1)} %bitcast.5) | data formatting | bytes 262144
  51.8 0.7 %copy.8 = f32[1,1,128,256]{3,2,1,0:T(8,128)} copy(f32[1,1,128,256]{3,2,1,0:T(8,128)S(1)} %bitcast.4) | data formatting | bytes 262144
Async XLA Ops:
  0.6 0.9 %copy-start = (bf16[32,2048]{1,0:T(8,128)(2,1)S(1)}, bf16[32,2048]{1,0:T(8,128)(2,1)}, u32[]{:S(2)}) copy-start(bf16[32,2048]{1,0:T(8,128)(2,1)} %param.3) | copy-start | bytes 393220

commit v4 on v3

--- a/solution.py
+++ b/solution.py
@@ -13,10 +13,10 @@
 SHAPE = (2, 8, 2, 4, 2, 2)
 FRAMES, LAG = 4096, 512
 NSEND = 99
-VMEM = 24 * 2**20
-
-
-def kernel(feats, inst, lagd, rows, cols, send, rsem, zsem, xsem, csem, hsem, ysem, osem):
+VMEM = 55_000_000
+
+
+def kernel(frames, freq, phases, inst, lagd, fbuf, wbuf, feats, ins, rows, cols, send, rsem, zsem, xsem, csem, hsem, ysem, osem):
     xl, zz, zp, y, xh, co = (lax.axis_index(a) for a in AXES)
     par, zq, up = zz % 2, zz // 2, zz // 4
     me_k = zp * 4 + y
@@ -56,6 +56,20 @@
     greet(xl=1 - xl)
     greet(xh=1 - xh)
     greet(co=1 - co)
+
+    loads = [pltpu.make_async_copy(frames, fbuf, ins.at[4])]
+    for j in range(4):
+        part = slice(256 * j, 256 * (j + 1))
+        loads.append(pltpu.make_async_copy(freq.at[:, part], wbuf.at[:, part], ins.at[j]))
+    for load in loads:
+        load.start()
+    loads[0].wait()
+    for j in range(4):
+        part = slice(256 * j, 256 * (j + 1))
+        loads[1 + j].wait()
+        projected = jnp.dot(fbuf[...], wbuf[:, part], preferred_element_type=jnp.float32)
+        projected += phases[:, part]
+        feats[:, part] = (SCALE * jnp.cos(projected)).astype(jnp.bfloat16)
     pl.semaphore_wait(barrier, 16 - own.astype(jnp.int32))
 
     for k in range(8):
@@ -203,17 +217,20 @@
 
 
 def shards(frames, frequency, phases):
-    projected = jnp.dot(frames, frequency, preferred_element_type=jnp.float32) + phases[None, :]
-    feats = (SCALE * jnp.cos(projected)).astype(jnp.bfloat16)
     vmem = pl.BlockSpec(memory_space=pltpu.VMEM)
+    hbm = pl.BlockSpec(memory_space=pltpu.HBM)
     dma = pltpu.SemaphoreType.DMA
     tile = jax.ShapeDtypeStruct((128, 256), jnp.float32)
     inst, lagd = pl.pallas_call(
         kernel,
         out_shape=(tile, tile),
-        in_specs=[vmem],
+        in_specs=[hbm, hbm, vmem],
         out_specs=(vmem, vmem),
         scratch_shapes=[
+            pltpu.VMEM(frames.shape, jnp.bfloat16),
+            pltpu.VMEM(frequency.shape, jnp.bfloat16),
+            pltpu.VMEM((32, 1024), jnp.bfloat16),
+            dma((5,)),
             pltpu.VMEM((4, 2, 2, 4, 2, 32, 128), jnp.bfloat16),
             pltpu.VMEM((4, 2, 2, 4, 2, 32, 256), jnp.bfloat16),
             dma((NSEND,)),
@@ -226,7 +243,7 @@
             dma,
         ],
         compiler_params=pltpu.CompilerParams(collective_id=0, has_side_effects=True, vmem_limit_bytes=VMEM),
-    )(feats)
+    )(frames, frequency, phases[None])
     return inst[None, None], lagd[None, None]
 
 

time: 52.6 us -> 50.8 us (0.966); the launches traced: 52.5 us -> 50 us
  matrix products: 3.42 us -> 0 us
  local copies, waits for them, and re-layouts: 2.22 us -> 2.9 us
    dot_general x1 -> x0, matrix products: 3.42 us -> none  [shards(): jnp.dot(frames, frequency, preferred_element_type=jnp.float32)]
    unnamed x4 -> x6, local copies, waits for them, and re-layouts: 2.22 us -> 2.9 us
where the time goes in v4:
time: 50.8 us; the launch traced here: 50 us
  Pallas kernels  46.5 us (92%)
  local copies, waits for them, and re-layouts  2.9 us (6%)
  between operations  0.65 us (1%)
    pallas_call x1, Pallas kernels, shards(): pl.pallas_call(kernel, out_shape=(tile, tile), in_specs=[hbm, hbm, vmem],...  46.5 us
    unnamed x6, local copies, waits for them, and re-layouts  2.9 us

profile of v4, /device:TPU:1, one launch (start us, length us, event | category | flops | bytes accessed | tf_op | source)
XLA Modules:
  0.0 50.0 jit_solution(390537365030509512)
XLA Ops:
  0.6 0.0 copy-start
  0.6 0.9 %copy-done = bf16[32,2048]{1,0:T(8,128)(2,1)S(1)} copy-done((bf16[32,2048]{1,0:T(8,128)(2,1)S(1)}, bf16[32,2048]{1,0:T(8,128)(2,1)}, u32[]{:S(2)}) %copy-start) | copy-done | bytes 131096
  1.5 0.0 copy-start.1
  1.5 0.7 %copy-done.1 = f32[1024]{0:T(1024)S(1)} copy-done((f32[1024]{0:T(1024)S(1)}, f32[1024]{0:T(1024)}, u32[]{:S(2)}) %copy-start.1) | copy-done | bytes 4120
  2.2 46.5 %shard_map.50 = (f32[128,256]{1,0:T(8,128)S(1)}, f32[128,256]{1,0:T(8,128)S(1)}) custom-call(bf16[32,2048]{1,0:T(8,128)(2,1)S(1)} %copy-done, bf16[2048,1024]{1,0:T(8,128)(2,1)} %freq.1, f32[1,1024]{1,0:T(1,128)S(1)} %bitcast.5), custom_call_target="tpu_custom_call" | custom-call | tf_op jit(solution)/shard_map/pallas_call | solution.py:224
  48.7 0.7 %copy.7 = f32[1,1,128,256]{3,2,1,0:T(8,128)} copy(f32[1,1,128,256]{3,2,1,0:T(8,128)S(1)} %bitcast.4) | data formatting | bytes 262144
  49.4 0.7 %copy.8 = f32[1,1,128,256]{3,2,1,0:T(8,128)} copy(f32[1,1,128,256]{3,2,1,0:T(8,128)S(1)} %bitcast.3) | data formatting | bytes 262144
Async XLA Ops:
  0.6 0.9 %copy-start = (bf16[32,2048]{1,0:T(8,128)(2,1)S(1)}, bf16[32,2048]{1,0:T(8,128)(2,1)}, u32[]{:S(2)}) copy-start(bf16[32,2048]{1,0:T(8,128)(2,1)} %frames.1) | copy-start | bytes 393220
  1.5 0.7 %copy-start.1 = (f32[1024]{0:T(1024)S(1)}, f32[1024]{0:T(1024)}, u32[]{:S(2)}) copy-start(f32[1024]{0:T(1024)} %param.5) | copy-start | bytes 12292

commit v5 on v4

--- a/solution.py
+++ b/solution.py
@@ -13,7 +13,7 @@
 SHAPE = (2, 8, 2, 4, 2, 2)
 FRAMES, LAG = 4096, 512
 NSEND = 99
-VMEM = 55_000_000
+VMEM = 56_200_000
 
 
 def kernel(frames, freq, phases, inst, lagd, fbuf, wbuf, feats, ins, rows, cols, send, rsem, zsem, xsem, csem, hsem, ysem, osem):
@@ -72,13 +72,6 @@
         feats[:, part] = (SCALE * jnp.cos(projected)).astype(jnp.bfloat16)
     pl.semaphore_wait(barrier, 16 - own.astype(jnp.int32))
 
-    for k in range(8):
-        src = feats.at[:, 128 * k : 128 * (k + 1)]
-        dst = rows.at[y, par, xl, zq, zp]
-        copy = remote(src, dst, rsem.at[y], zp=k // 4, y=k % 4)
-        local = pltpu.make_async_copy(src, dst, rsem.at[y])
-        pl.when(me_k != k)(copy.start)
-        pl.when(me_k == k)(local.start)
     for j in range(4):
         src = feats.at[:, 256 * j : 256 * (j + 1)]
         dst = cols.at[y, par, xl, zq, zp]
@@ -87,6 +80,13 @@
         local = pltpu.make_async_copy(src, dst, csem.at[zq])
         pl.when(jnp.logical_not(mine))(copy.start)
         pl.when(mine)(local.start)
+    for k in range(8):
+        src = feats.at[:, 128 * k : 128 * (k + 1)]
+        dst = rows.at[y, par, xl, zq, zp]
+        copy = remote(src, dst, rsem.at[y], zp=k // 4, y=k % 4)
+        local = pltpu.make_async_copy(src, dst, rsem.at[y])
+        pl.when(me_k != k)(copy.start)
+        pl.when(me_k == k)(local.start)
 
     def push(ref, sem, **dev):
         remote(ref, ref, sem, **dev).start()
@@ -126,8 +126,8 @@
     nxt, prv, opp = (y + 1) % 4, (y + 3) % 4, (y + 2) % 4
     piece = [(zq + d) % 4 for d in (0, 1, 3, 2)]
 
-    def other(v, p):
-        push(cols.at[v, co, :, piece[p]], osem, co=1 - co)
+    def other(d, p):
+        push(cols.at[(y + d) % 4, co, :, piece[p]], osem.at[d], co=1 - co)
 
     def col_x(p):
         q = piece[p]
@@ -145,7 +145,7 @@
         for h in range(2):
             push(cols.at[y, co, h, q], ysem.at[0, p, h], y=nxt)
             push(cols.at[y, co, 1 - h, q], ysem.at[1, p, 1 - h], y=prv)
-        other(y, p)
+        other(0, p)
 
     def col_far(p):
         q = piece[p]
@@ -154,63 +154,67 @@
         arrived(cols.at[nxt, co, 1, q], ysem.at[1, p, 1])
         push(cols.at[nxt, co, 1, q], ysem.at[1, p, 2], y=prv)
         arrived(cols.at[prv, co, 1, q], ysem.at[0, p, 1])
-        other(prv, p)
+        other(3, p)
         arrived(cols.at[nxt, co, 0, q], ysem.at[1, p, 0])
-        other(nxt, p)
+        other(1, p)
 
     def col_last(p):
         q = piece[p]
         arrived(cols.at[opp, co, 0, q], ysem.at[0, p, 2])
         arrived(cols.at[opp, co, 1, q], ysem.at[1, p, 2])
-        other(opp, p)
+        other(2, p)
 
     row_start()
-    col_x(0)
-    col_x(1)
-    col_x(2)
+    for p in range(4):
+        col_x(p)
+    col_z(0)
     row_step(1)
-    col_z(0)
-    col_x(3)
     col_z(1)
     col_z(2)
     col_y(0)
-    row_step(2)
     col_z(3)
     col_y(1)
+    row_step(2)
     col_y(2)
+    col_y(3)
     col_far(0)
-    row_step(3)
-    col_y(3)
     col_far(1)
     col_far(2)
+    row_step(3)
     col_last(0)
+    col_far(3)
+    col_last(1)
     row_last()
-    col_far(3)
-    for p in range(1, 4):
-        col_last(p)
+    col_last(2)
+    col_last(3)
     arrived(rows.at[:, :, 1 - xl], xsem)
-    arrived(cols.at[:, 1 - co], osem)
 
     over = (((0,), (0,)), ((), ()))
 
-    def body(i, carry):
+    def add(d, side, carry):
         total, late = carry
-        r = rows[i // 2, i % 2].reshape(512, 128)
-        c = cols[i // 2, i % 2].reshape(512, 256)
+        v = (y + d) % 4
+        r = rows[v, side].reshape(512, 128)
+        c = cols[v, side].reshape(512, 256)
         total += lax.dot_general(r, c, over, preferred_element_type=jnp.float32)
         late += lax.dot_general(r[:448], c[64:], over, preferred_element_type=jnp.float32)
         return total, late
 
+    def others(d, carry):
+        arrived(cols.at[(y + d) % 4, 1 - co], osem.at[d])
+        return add(d, 1 - co, carry)
+
     zero = jnp.zeros(inst.shape, jnp.float32)
-    total, late = lax.fori_loop(0, 8, body, (zero, zero))
+    sums = lax.fori_loop(0, 4, lambda d, carry: add(d, co, carry), (zero, zero))
+    total, late = lax.fori_loop(0, 4, others, sums)
     inst[...] = total / FRAMES
     lagd[...] = late / (FRAMES - LAG)
 
-    for k, copy in enumerate(sends[:8]):
-        pl.when(me_k != k)(copy.wait_send)
-    for j, copy in enumerate(sends[8:12]):
+    for j, copy in enumerate(sends[:4]):
         mine = jnp.logical_and(own, zz == 4 * co + j)
         pl.when(jnp.logical_not(mine))(copy.wait_send)
+    for k, copy in enumerate(sends[4:12]):
+        pl.when(me_k != k)(copy.wait_send)
     assert len(sends) == NSEND
     for copy in sends[12:]:
         copy.wait_send()
@@ -240,7 +244,7 @@
             dma((4,)),
             dma((2, 4)),
             dma((2, 4, 3)),
-            dma,
+            dma((4,)),
         ],
         compiler_params=pltpu.CompilerParams(collective_id=0, has_side_effects=True, vmem_limit_bytes=VMEM),
     )(frames, frequency, phases[None])

time: 50.8 us -> 50.8 us (level)
  the two profiles are of different devices: /device:TPU:1 before, /device:TPU:4 now
where the time goes in v5:
time: 50.8 us; the launch traced here: 50.7 us
  Pallas kernels  48 us (94%)
  local copies, waits for them, and re-layouts  1.99 us (4%)
  between operations  0.65 us (1%)
    pallas_call x1, Pallas kernels, shards(): pl.pallas_call(kernel, out_shape=(tile, tile), in_specs=[hbm, hbm, vmem],...  48 us
    unnamed x4, local copies, waits for them, and re-layouts  1.99 us

profile of v5, /device:TPU:4, one launch (start us, length us, event | category | flops | bytes accessed | tf_op | source)
XLA Modules:
  0.0 50.7 jit_solution(4849152241506655355)
XLA Ops:
  0.6 0.0 copy-start
  0.6 0.7 %copy-done = f32[1024]{0:T(1024)S(1)} copy-done((f32[1024]{0:T(1024)S(1)}, f32[1024]{0:T(1024)}, u32[]{:S(2)}) %copy-start) | copy-done | bytes 4120
  1.3 48.0 %shard_map.50 = (f32[128,256]{1,0:T(8,128)S(1)}, f32[128,256]{1,0:T(8,128)S(1)}) custom-call(bf16[32,2048]{1,0:T(8,128)(2,1)} %frames.1, bf16[2048,1024]{1,0:T(8,128)(2,1)} %freq.1, f32[1,1024]{1,0:T(1,128)S(1)} %bitcast.5), custom_call_target="tpu_custom_call" | custom-call | tf_op jit(solution)/shard_map/pallas_call | solution.py:228
  49.3 0.7 %copy.7 = f32[1,1,128,256]{3,2,1,0:T(8,128)} copy(f32[1,1,128,256]{3,2,1,0:T(8,128)S(1)} %bitcast.4) | data formatting | bytes 262144
  50.0 0.7 %copy.8 = f32[1,1,128,256]{3,2,1,0:T(8,128)} copy(f32[1,1,128,256]{3,2,1,0:T(8,128)S(1)} %bitcast.3) | data formatting | bytes 262144
Async XLA Ops:
  0.6 0.7 %copy-start = (f32[1024]{0:T(1024)S(1)}, f32[1024]{0:T(1024)}, u32[]{:S(2)}) copy-start(f32[1024]{0:T(1024)} %param.5) | copy-start | bytes 12292

commit v6 on v5

--- a/solution.py
+++ b/solution.py
@@ -72,6 +72,13 @@
         feats[:, part] = (SCALE * jnp.cos(projected)).astype(jnp.bfloat16)
     pl.semaphore_wait(barrier, 16 - own.astype(jnp.int32))
 
+    for k in range(8):
+        src = feats.at[:, 128 * k : 128 * (k + 1)]
+        dst = rows.at[y, par, xl, zq, zp]
+        copy = remote(src, dst, rsem.at[y], zp=k // 4, y=k % 4)
+        local = pltpu.make_async_copy(src, dst, rsem.at[y])
+        pl.when(me_k != k)(copy.start)
+        pl.when(me_k == k)(local.start)
     for j in range(4):
         src = feats.at[:, 256 * j : 256 * (j + 1)]
         dst = cols.at[y, par, xl, zq, zp]
@@ -80,13 +87,6 @@
         local = pltpu.make_async_copy(src, dst, csem.at[zq])
         pl.when(jnp.logical_not(mine))(copy.start)
         pl.when(mine)(local.start)
-    for k in range(8):
-        src = feats.at[:, 128 * k : 128 * (k + 1)]
-        dst = rows.at[y, par, xl, zq, zp]
-        copy = remote(src, dst, rsem.at[y], zp=k // 4, y=k % 4)
-        local = pltpu.make_async_copy(src, dst, rsem.at[y])
-        pl.when(me_k != k)(copy.start)
-        pl.when(me_k == k)(local.start)
 
     def push(ref, sem, **dev):
         remote(ref, ref, sem, **dev).start()
@@ -167,26 +167,18 @@
     row_start()
     for p in range(4):
         col_x(p)
-    col_z(0)
     row_step(1)
-    col_z(1)
-    col_z(2)
-    col_y(0)
-    col_z(3)
-    col_y(1)
+    for p in range(4):
+        col_z(p)
     row_step(2)
-    col_y(2)
-    col_y(3)
-    col_far(0)
-    col_far(1)
-    col_far(2)
+    for p in range(4):
+        col_y(p)
     row_step(3)
-    col_last(0)
-    col_far(3)
-    col_last(1)
     row_last()
-    col_last(2)
-    col_last(3)
+    for p in range(4):
+        col_far(p)
+    for p in range(4):
+        col_last(p)
     arrived(rows.at[:, :, 1 - xl], xsem)
 
     over = (((0,), (0,)), ((), ()))
@@ -210,10 +202,10 @@
     inst[...] = total / FRAMES
     lagd[...] = late / (FRAMES - LAG)
 
-    for j, copy in enumerate(sends[:4]):
+    for j, copy in enumerate(sends[8:12]):
         mine = jnp.logical_and(own, zz == 4 * co + j)
         pl.when(jnp.logical_not(mine))(copy.wait_send)
-    for k, copy in enumerate(sends[4:12]):
+    for k, copy in enumerate(sends[:8]):
         pl.when(me_k != k)(copy.wait_send)
     assert len(sends) == NSEND
     for copy in sends[12:]:

time: 50.8 us -> 49.5 us (0.974)
  the two profiles are of different devices: /device:TPU:4 before, /device:TPU:1 now
where the time goes in v6:
time: 49.5 us; the launch traced here: 49.4 us
  Pallas kernels  46.7 us (94%)
  local copies, waits for them, and re-layouts  1.99 us (4%)
  between operations  0.65 us (1%)
    pallas_call x1, Pallas kernels, shards(): pl.pallas_call(kernel, out_shape=(tile, tile), in_specs=[hbm, hbm, vmem],...  46.7 us
    unnamed x4, local copies, waits for them, and re-layouts  1.99 us

profile of v6, /device:TPU:1, one launch (start us, length us, event | category | flops | bytes accessed | tf_op | source)
XLA Modules:
  0.0 49.4 jit_solution(3139746494231295731)
XLA Ops:
  0.6 0.0 copy-start
  0.6 0.7 %copy-done = f32[1024]{0:T(1024)S(1)} copy-done((f32[1024]{0:T(1024)S(1)}, f32[1024]{0:T(1024)}, u32[]{:S(2)}) %copy-start) | copy-done | bytes 4120
  1.3 46.7 %shard_map.50 = (f32[128,256]{1,0:T(8,128)S(1)}, f32[128,256]{1,0:T(8,128)S(1)}) custom-call(bf16[32,2048]{1,0:T(8,128)(2,1)} %frames.1, bf16[2048,1024]{1,0:T(8,128)(2,1)} %freq.1, f32[1,1024]{1,0:T(1,128)S(1)} %bitcast.5), custom_call_target="tpu_custom_call" | custom-call | tf_op jit(solution)/shard_map/pallas_call | solution.py:220
  48.1 0.7 %copy.7 = f32[1,1,128,256]{3,2,1,0:T(8,128)} copy(f32[1,1,128,256]{3,2,1,0:T(8,128)S(1)} %bitcast.4) | data formatting | bytes 262144
  48.7 0.7 %copy.8 = f32[1,1,128,256]{3,2,1,0:T(8,128)} copy(f32[1,1,128,256]{3,2,1,0:T(8,128)S(1)} %bitcast.3) | data formatting | bytes 262144
Async XLA Ops:
  0.6 0.7 %copy-start = (f32[1024]{0:T(1024)S(1)}, f32[1024]{0:T(1024)}, u32[]{:S(2)}) copy-start(f32[1024]{0:T(1024)} %param.5) | copy-start | bytes 12292

commit v7 on v6

--- a/solution.py
+++ b/solution.py
@@ -174,9 +174,9 @@
     for p in range(4):
         col_y(p)
     row_step(3)
+    for p in range(4):
+        col_far(p)
     row_last()
-    for p in range(4):
-        col_far(p)
     for p in range(4):
         col_last(p)
     arrived(rows.at[:, :, 1 - xl], xsem)

time: 49.5 us -> 48 us (0.970)
  the two profiles are of different devices: /device:TPU:1 before, /device:TPU:32 now
where the time goes in v7:
time: 48 us; the launch traced here: 47.9 us
  Pallas kernels  45.2 us (94%)
  local copies, waits for them, and re-layouts  1.99 us (4%)
  between operations  0.65 us (1%)
    pallas_call x1, Pallas kernels, shards(): pl.pallas_call(kernel, out_shape=(tile, tile), in_specs=[hbm, hbm, vmem],...  45.2 us
    unnamed x4, local copies, waits for them, and re-layouts  1.99 us

profile of v7, /device:TPU:32, one launch (start us, length us, event | category | flops | bytes accessed | tf_op | source)
XLA Modules:
  0.0 47.9 jit_solution(10261648193837570104)
XLA Ops:
  0.6 0.0 copy-start
  0.6 0.7 %copy-done = f32[1024]{0:T(1024)S(1)} copy-done((f32[1024]{0:T(1024)S(1)}, f32[1024]{0:T(1024)}, u32[]{:S(2)}) %copy-start) | copy-done | bytes 4120
  1.3 45.2 %shard_map.50 = (f32[128,256]{1,0:T(8,128)S(1)}, f32[128,256]{1,0:T(8,128)S(1)}) custom-call(bf16[32,2048]{1,0:T(8,128)(2,1)} %frames.1, bf16[2048,1024]{1,0:T(8,128)(2,1)} %freq.1, f32[1,1024]{1,0:T(1,128)S(1)} %bitcast.5), custom_call_target="tpu_custom_call" | custom-call | tf_op jit(solution)/shard_map/pallas_call | solution.py:220
  46.5 0.7 %copy.7 = f32[1,1,128,256]{3,2,1,0:T(8,128)} copy(f32[1,1,128,256]{3,2,1,0:T(8,128)S(1)} %bitcast.4) | data formatting | bytes 262144
  47.2 0.7 %copy.8 = f32[1,1,128,256]{3,2,1,0:T(8,128)} copy(f32[1,1,128,256]{3,2,1,0:T(8,128)S(1)} %bitcast.3) | data formatting | bytes 262144
Async XLA Ops:
  0.6 0.7 %copy-start = (f32[1024]{0:T(1024)S(1)}, f32[1024]{0:T(1024)}, u32[]{:S(2)}) copy-start(f32[1024]{0:T(1024)} %param.5) | copy-start | bytes 12292
